TPU v7x, 32 devices: a whole 2x2x4 slice. The times are simulated.
32 devices in a mesh: group: 2 (over x), dom: 16 (over z, y, core).
Axes of the slice: x: 2, y: 2, z: 4, core: 2. Of those that a mesh axis runs over, the one named last changes fastest.
Arguments:
- features: bfloat16 [8192, 512], P(('group', 'dom')), may hold values from -6 to 6
- tile_columns: int32 [32, 2, 4], P(('group', 'dom')), may hold values from 0 to 1
- tile_values: bfloat16 [32, 2, 4, 128, 128], P(('group', 'dom')), as said below
- send_rows: int32 [32, 16, 16], P(('group', 'dom')), may hold values from 0 to 255
- send_count: int32 [32, 16], P(('group', 'dom')), may hold values from 0 to 16, as said below
- ghost_target: int32 [32, 16, 16], P(('group', 'dom')), may hold values from 0 to 255
- query_rows: int32 [32, 512], P(('group', 'dom')), may hold values from 0 to 255
- positive_cand: int32 [32, 512], P(('group', 'dom')), may hold values from 0 to 63
- negative_rows: int32 [32, 32], P(('group', 'dom')), may hold values from 0 to 255
- weight_self: bfloat16 [512, 512], replicated, may hold values from -0.25 to 0.25
- weight_neigh: bfloat16 [512, 512], replicated, may hold values from -0.75 to 0.75
Outputs:
- embeddings: bfloat16 [8192, 512], P(('group', 'dom'))
- weight_grads: bfloat16 [1024, 512], P('dom')
Inputs may be any that keep to these rules, and one draw needn't show every extreme that they name: `send_count`: no device sends rows to its own index of dom; in every group one index of dom receives exactly 16 rows from every other index. `tile_values`: weights are zero or between 0.5 and 1.
All inputs are finite; a program needn't handle non-finite values.
Results may differ from a plain program's by a relative error of at most 0.015.
Values may be sent and summed in bfloat16 or wider, within the bound.
No kernel may reach another device: no remote copies, remote signals or barrier semaphores. Data moves between devices by JAX's collectives and lax.ppermute only.
A program may use at most 64 MiB of HBM per device.

v0:
```python
import math
import jax
import jax.numpy as jnp
from jax import lax
from jax.sharding import PartitionSpec as P

LOSS_FACTOR = 64.0
EPSILON = 1e-05


def score_grads(scores, positive, cand_total, query_total):
    sigma = jax.nn.sigmoid(scores)
    dscore = jnp.where(positive, sigma - 1.0, sigma / (cand_total - 1.0)) * (
        LOSS_FACTOR / query_total
    )
    return dscore.astype(jnp.bfloat16)


def transpose_dot(left, right):
    return lax.dot_general(
        left, right, (((0,), (0,)), ((), ())), preferred_element_type=jnp.float32
    )


def on_device(
    features,
    tile_columns,
    tile_values,
    send_rows,
    send_count,
    ghost_target,
    query_rows,
    positive_cand,
    negative_rows,
    weight_self,
    weight_neigh,
):
    node_count, width = features.shape
    row_blocks, tiles_row, tile_size = (
        tile_values.shape[1],
        tile_values.shape[2],
        tile_values.shape[3],
    )
    slot_count = send_rows.shape[2]
    group_count = lax.axis_size("group")
    score_factor = 1.0 / math.sqrt(width)
    outgoing = features[send_rows[0]]
    flags = (jnp.arange(slot_count, dtype=jnp.int32)[None, :] < send_count[0][:, None]).astype(
        jnp.bfloat16
    )
    received, flags_in = (
        lax.all_to_all(outgoing, "dom", split_axis=0, concat_axis=0, tiled=True),
        lax.all_to_all(flags, "dom", split_axis=0, concat_axis=0, tiled=True),
    )
    blocks = features.reshape(row_blocks, tile_size, width)
    picked = blocks[tile_columns[0]]
    local = jnp.einsum(
        "rtij,rtjd->rid", tile_values[0], picked, preferred_element_type=jnp.float32
    ).reshape(node_count, width)
    row_weight = jnp.sum(tile_values[0].astype(jnp.float32), axis=(1, 3)).reshape(node_count)
    live = flags_in.astype(jnp.float32)
    targets = ghost_target[0].reshape(-1)
    weighted = (received.astype(jnp.float32) * live[:, :, None]).reshape(-1, width)
    ghost_sum = jnp.zeros((node_count, width), jnp.float32).at[targets].add(weighted)
    ghost_count = jnp.zeros((node_count,), jnp.float32).at[targets].add(live.reshape(-1))
    degree = 1.0 + row_weight + ghost_count
    aggregate = ((local + ghost_sum) / degree[:, None]).astype(jnp.bfloat16)
    pre = jnp.dot(features, weight_self, preferred_element_type=jnp.float32) + jnp.dot(
        aggregate, weight_neigh, preferred_element_type=jnp.float32
    )
    scale = lax.rsqrt(jnp.mean(pre * pre, axis=-1, keepdims=True) + EPSILON)
    embeds = (pre * scale).astype(jnp.bfloat16)
    queries = embeds[query_rows[0]]
    own_negs = embeds[negative_rows[0]]
    neg_count = own_negs.shape[0]
    query_total = queries.shape[0]
    cand_total = neg_count * group_count
    targets_pos = positive_cand[0][:, None]
    all_negs = lax.all_gather(own_negs, "group", axis=0, tiled=True)
    scores = score_factor * jnp.dot(queries, all_negs.T, preferred_element_type=jnp.float32)
    positive = targets_pos == jnp.arange(cand_total, dtype=jnp.int32)[None, :]
    dscore = score_grads(scores, positive, cand_total, query_total)
    query_grad = score_factor * jnp.dot(dscore, all_negs, preferred_element_type=jnp.float32)
    neg_grad = lax.psum_scatter(
        (score_factor * transpose_dot(dscore, queries)).astype(jnp.bfloat16),
        "group",
        scatter_dimension=0,
        tiled=True,
    ).astype(jnp.float32)
    emb_grad = jnp.zeros((node_count, width), jnp.float32)
    emb_grad = emb_grad.at[query_rows[0]].add(query_grad)
    emb_grad = emb_grad.at[negative_rows[0]].add(neg_grad)
    inner = jnp.mean(pre * emb_grad, axis=-1, keepdims=True)
    pre_grad = (scale * emb_grad - pre * scale * scale * scale * inner).astype(jnp.bfloat16)
    stacked = jnp.concatenate([features, aggregate], axis=1)
    shard = lax.psum_scatter(
        transpose_dot(stacked, pre_grad), "dom", scatter_dimension=0, tiled=True
    )
    summed = lax.psum(shard.astype(jnp.bfloat16), "group")
    return (embeds, summed)


def solution(mesh):
    placed = (
        P(("group", "dom"), None),
        P(("group", "dom"), None, None),
        P(("group", "dom"), None, None, None, None),
        P(("group", "dom"), None, None),
        P(("group", "dom"), None),
        P(("group", "dom"), None, None),
        P(("group", "dom"), None),
        P(("group", "dom"), None),
        P(("group", "dom"), None),
        P(),
        P(),
    )
    return jax.shard_map(
        on_device,
        mesh=mesh,
        in_specs=placed,
        out_specs=(P(("group", "dom"), None), P("dom", None)),
        check_vma=False,
    )
```

profile of v0, /device:TPU:0, one launch (start us, length us, event | category | flops | bytes accessed | tf_op | source)
XLA Modules:
  0.0 157.0 jit_solution(12821754926774188139)
XLA Ops:
  7.2 0.0 copy-start
  7.2 0.0 copy-start.2
  7.2 1.4 compare_convert_fusion
  8.6 7.4 %all-to-all-start.1 = ((bf16[16,1,16]{2,1,0:T(2,128)(2,1)}), bf16[16,1,16]{2,1,0:T(2,128)(2,1)S(1)}, u32[]{:S(2)}, u32[]{:S(2)}) async-start(bf16[16,1,16]{2,1,0:T(2,128)(2,1)} %compare_convert_fusion), calls=%async_computation.1 | async-start | bytes 16384 | tf_op jit(solution)/shard_map/all_to_all | solution.py:53
  16.0 0.7 fusion.17
  16.7 0.7 compare_select_fusion.3
  17.4 0.1 reshape.231
  17.4 0.8 reshape_squeeze.3
  18.2 1.1 convert_reduce_fusion
  19.3 0.7 compare_select_fusion.1
  20.0 0.7 compare_select_fusion
  20.7 0.1 reshape.239
  20.8 1.4 fusion.19
  22.2 0.0 copy-done.2
  22.3 0.0 copy-start.3
  22.3 1.9 %gather_fusion.1 = bf16[256,512]{1,0:T(8,128)(2,1)} fusion(bf16[256,512]{1,0:T(8,128)(2,1)S(1)} %copy-done.2, s32[1024]{0:T(1024)S(1)} %pad_clamp_fusion.2), kind=kCustom, calls=%fused_computation.1 | custom fusion | bytes 525312 | tf_op jit(solution)/shard_map/gather | solution.py:47
  24.1 0.6 gather_fusion
  24.7 0.0 all-to-all-done.1
  24.8 6.0 %all-to-all-start = ((bf16[16,16,512]{2,1,0:T(8,128)(2,1)}), bf16[16,16,512]{2,1,0:T(8,128)(2,1)S(1)}, u32[]{:S(2)}, u32[]{:S(2)}) async-start(bf16[16,16,512]{2,1,0:T(8,128)(2,1)} %bitcast.10), calls=%async_computation | async-start | bytes 524288 | tf_op jit(solution)/shard_map/all_to_all | solution.py:52
  30.8 0.0 reduce-scatter.3.cloned.1.call-start
  30.8 0.0 copy-done.3
  30.9 0.3 fusion.9
  31.2 0.1 reshape.273
  31.3 2.3 %scatter_fusion.1 = f32[256]{0:T(256)S(1)} fusion(f32[256]{0:T(256)S(1)} %add_bitcast_fusion, s32[256]{0:T(256)S(1)} %bitcast.51, f32[256]{0:T(256)S(1)} %reshape.273), kind=kCustom, calls=%fused_computation.5 | custom fusion | flops 256 | bytes 4096 | tf_op jit(solution)/shard_map/scatter-add | solution.py:65
  33.6 7.2 %all-to-all-done = bf16[16,16,512]{2,1,0:T(8,128)(2,1)S(1)} async-done(((bf16[16,16,512]{2,1,0:T(8,128)(2,1)}), bf16[16,16,512]{2,1,0:T(8,128)(2,1)S(1)}, u32[]{:S(2)}, u32[]{:S(2)}) %all-to-all-start) | async-done | bytes 262176 | tf_op jit(solution)/shard_map/all_to_all | solution.py:52
  40.8 0.1 convert_multiply_fusion
  40.9 2.3 %scatter_fusion = f32[256,512]{1,0:T(8,128)S(1)} fusion(f32[256,512]{1,0:T(8,128)S(1)} %bitcast.46, s32[256]{0:T(256)S(1)} %bitcast.52, f32[256,512]{1,0:T(8,128)S(1)} %bitcast.49), kind=kCustom, calls=%fused_computation.4 | custom fusion | flops 131072 | bytes 1573888 | tf_op jit(solution)/shard_map/scatter-add | solution.py:64
  43.2 0.1 divide_convert_fusion
  43.3 0.0 copy-done
  43.3 0.4 multiply_reduce_fusion.1
  43.7 0.1 multiply_convert_fusion
  43.9 0.0 copy-start.1
  43.9 0.6 gather_fusion.3
  44.5 4.6 %all-gather = bf16[64,512]{1,0:T(8,128)(2,1)S(1)} all-gather(bf16[32,512]{1,0:T(8,128)(2,1)S(1)} %gather_fusion.3), channel_id=2, replica_groups=mesh['group'=2,'dom'=16] {'group'}, dimensions={0}, use_global_device_ids=true | all-gather | bytes 98304 | tf_op jit(solution)/shard_map/all_gather | solution.py:79
  49.1 0.0 copy-start.4
  49.1 2.0 %gather_fusion.2 = bf16[512,512]{1,0:T(8,128)(2,1)S(1)} fusion(bf16[256,512]{1,0:T(8,128)(2,1)S(1)} %multiply_convert_fusion, s32[1024]{0:T(1024)S(1)} %pad_clamp_fusion.1), kind=kCustom, calls=%fused_computation.2 | custom fusion | bytes 1050624 | tf_op jit(solution)/shard_map/gather | solution.py:73
  51.1 0.0 copy-done.1
  51.1 0.0 copy-done.4
  51.1 0.3 multiply_convert_fusion.1
  51.4 0.8 fusion.4
  52.3 0.0 reduce-scatter.3.cloned.1.call-update
  52.3 0.0 reduce-scatter.5.cloned.1.call-start
  52.3 0.3 convolution_multiply_fusion
  52.6 3.7 %scatter_custom_fusion.2 = f32[256,512]{1,0:T(8,128)S(1)} fusion(s32[512]{0:T(512)S(1)} %bitcast.54, f32[512,512]{1,0:T(8,128)S(1)} %convolution_multiply_fusion, f32[]{:T(128)} %constant.14.clone.1), kind=kCustom, calls=%fused_computation.31 | custom fusion | flops 262144 | bytes 524292 | tf_op jit(solution)/shard_map/scatter-add | solution.py:91
  56.4 4.3 %reduce-scatter.3.cloned.1.call-done = bf16[32,512]{1,0:T(8,128)(2,1)} async-done(((bf16[64,512]{1,0:T(8,128)(2,1)}), bf16[32,512]{1,0:T(8,128)(2,1)}) %reduce-scatter.3.cloned.1.call-update) | async-done | bytes 32784 | tf_op jit(solution)/shard_map/reduce_scatter | solution.py:84
  60.6 1.2 scatter_custom_fusion.3
  61.9 0.1 multiply_reduce_fusion
  62.0 2.0 %fusion.5 = f32[1024,512]{1,0:T(8,128)} fusion(bf16[256,512]{1,0:T(8,128)(2,1)S(1)} %divide_convert_fusion, bf16[256,512]{1,0:T(8,128)(2,1)S(1)} %copy-done.2, f32[256,512]{1,0:T(8,128)S(1)} %scatter_custom_fusion.3, f32[256,512]{1,0:T(8,128)S(1)} %get-tuple-element.3, f32[256]{0:T(256)S(1)} %broadcast_multiply_fusion, f32[256]{0:T(256)S(1)} %add_rsqrt_fusion), kind=kOutput, calls=%fused_computation.17 | convolution fusion | flops 270401536 | bytes 3672064 | tf_op jit(solution)/shard_map/dot_general | solution.py:20
  64.0 0.0 reduce-scatter.5.cloned.1.call-update
  64.0 0.0 all-reduce.2.cloned.1.call-start
  64.0 62.2 %reduce-scatter.5.cloned.1.call-done = f32[64,512]{1,0:T(8,128)} async-done(((f32[1024,512]{1,0:T(8,128)}), f32[64,512]{1,0:T(8,128)}) %reduce-scatter.5.cloned.1.call-update) | async-done | bytes 131088 | tf_op jit(solution)/shard_map/reduce_scatter | solution.py:96
  126.2 1.5 convert_element_type.66
  127.8 0.0 all-reduce.2.cloned.1.call-update
  127.8 21.2 %all-reduce.2.cloned.1.call-done = bf16[64,512]{1,0:T(8,128)(2,1)} async-done(((bf16[64,512]{1,0:T(8,128)(2,1)}), bf16[64,512]{1,0:T(8,128)(2,1)}) %all-reduce.2.cloned.1.call-update) | async-done | bytes 65552 | tf_op jit(solution)/shard_map/psum | solution.py:99
  149.0 1.5 copy.18
  (10 shorter events, 0.1 us)
Async XLA Ops:
  7.2 36.2 %copy-start = (bf16[512,512]{1,0:T(8,128)(2,1)S(1)}, bf16[512,512]{1,0:T(8,128)(2,1)}, u32[]{:S(2)}) copy-start(bf16[512,512]{1,0:T(8,128)(2,1)} %param.21) | copy-start | bytes 1572868
  7.2 15.1 %copy-start.2 = (bf16[256,512]{1,0:T(8,128)(2,1)S(1)}, bf16[256,512]{1,0:T(8,128)(2,1)}, u32[]{:S(2)}) copy-start(bf16[256,512]{1,0:T(8,128)(2,1)} %param.11) | copy-start | bytes 786436
  8.6 16.1 %all-to-all-start.1 = ((bf16[16,1,16]{2,1,0:T(2,128)(2,1)}), bf16[16,1,16]{2,1,0:T(2,128)(2,1)S(1)}, u32[]{:S(2)}, u32[]{:S(2)}) async-start(bf16[16,1,16]{2,1,0:T(2,128)(2,1)} %compare_convert_fusion), calls=%async_computation.1 | async-start | bytes 16384 | tf_op jit(solution)/shard_map/all_to_all | solution.py:53
  22.3 8.6 %copy-start.3 = (bf16[1,2,4,128,128]{4,3,2,1,0:T(8,128)(2,1)S(1)}, bf16[1,2,4,128,128]{4,3,2,1,0:T(8,128)(2,1)}, u32[]{:S(2)}) copy-start(bf16[1,2,4,128,128]{4,3,2,1,0:T(8,128)(2,1)} %param.13) | copy-start | bytes 786436
  24.8 16.0 %all-to-all-start = ((bf16[16,16,512]{2,1,0:T(8,128)(2,1)}), bf16[16,16,512]{2,1,0:T(8,128)(2,1)S(1)}, u32[]{:S(2)}, u32[]{:S(2)}) async-start(bf16[16,16,512]{2,1,0:T(8,128)(2,1)} %bitcast.10), calls=%async_computation | async-start | bytes 524288 | tf_op jit(solution)/shard_map/all_to_all | solution.py:52
  30.8 29.9 %reduce-scatter.3.cloned.1.call-start = ((), (), s32[]{:S(2)}) async-start(), calls=%async_computation.4 | async-start | bytes 98304 | tf_op jit(solution)/shard_map/reduce_scatter | solution.py:84
  43.9 7.2 %copy-start.1 = (bf16[256,512]{1,0:T(8,128)(2,1)}, bf16[256,512]{1,0:T(8,128)(2,1)S(1)}, u32[]{:S(2)}) copy-start(bf16[256,512]{1,0:T(8,128)(2,1)S(1)} %multiply_convert_fusion) | copy-start | bytes 786436
  49.1 2.0 %copy-start.4 = (s32[1,512]{1,0:T(1,128)S(1)}, s32[1,512]{1,0:T(1,128)}, u32[]{:S(2)}) copy-start(s32[1,512]{1,0:T(1,128)} %param.18) | copy-start | bytes 6148
  52.3 74.0 %reduce-scatter.5.cloned.1.call-start = ((), (), s32[]{:S(2)}) async-start(), calls=%async_computation.5 | async-start | bytes 2228224 | tf_op jit(solution)/shard_map/reduce_scatter | solution.py:96
  64.0 85.0 %all-reduce.2.cloned.1.call-start = ((), (), s32[]{:S(2)}) async-start(), calls=%async_computation.6 | async-start | bytes 131072 | tf_op jit(solution)/shard_map/psum | solution.py:99
Sparse Core Ops, SparseCore 0:
  52.4 8.1 reduce-scatter.2
  64.4 61.8 reduce-scatter.4
  129.1 19.8 all-reduce.1
where the time goes:
time: 158 us; the launch traced here: 157 us
  waiting for transfers between devices  94.9 us (60%)
  other arithmetic  16.8 us (11%)
  between operations  14 us (9%)
  starting transfers between devices  13.6 us (9%)
  local copies, waits for them, and re-layouts  7.58 us (5%)
  matrix products  5.54 us (4%)
  blocking collectives  4.58 us (3%)
    reduce_scatter x1, waiting for transfers between devices, on_device(): lax.psum_scatter(transpose_dot(stacked, pre_grad), 'dom', scatter_dimensi...  62.2 us
    psum x1, waiting for transfers between devices, on_device(): summed = lax.psum(shard.astype(jnp.bfloat16), 'group')  21.2 us
    all_to_all x1, starting transfers between devices, on_device(): lax.all_to_all(flags, 'dom', split_axis=0, concat_axis=0, tiled=True)  7.41 us
    all_to_all x1, waiting for transfers between devices, on_device(): lax.all_to_all(outgoing, 'dom', split_axis=0, concat_axis=0, tiled=True)  7.18 us
    all_to_all x1, starting transfers between devices, on_device(): lax.all_to_all(outgoing, 'dom', split_axis=0, concat_axis=0, tiled=True)  6.02 us
    all_gather x1, blocking collectives, on_device(): all_negs = lax.all_gather(own_negs, 'group', axis=0, tiled=True)  4.58 us
    reduce_scatter x1, waiting for transfers between devices, on_device(): lax.psum_scatter((score_factor * transpose_dot(dscore, queries)).astype(j...  4.28 us
    scatter-add x1, other arithmetic, on_device(): emb_grad = emb_grad.at[query_rows[0]].add(query_grad)  3.71 us
  transfers between devices with their start and end apart: 5, of which 4 were waited for; matrix products, arithmetic and copies ran while one was open for 10% of the time, Pallas kernels for 0%

commit v1 on v0

--- a/solution.py
+++ b/solution.py
@@ -96,7 +96,7 @@
     shard = lax.psum_scatter(
         transpose_dot(stacked, pre_grad), "dom", scatter_dimension=0, tiled=True
     )
-    summed = lax.psum(shard.astype(jnp.bfloat16), "group")
+    summed = jnp.sum(lax.all_gather(shard.astype(jnp.bfloat16), "group"), axis=0)
     return (embeds, summed)
 
 

time: 158 us -> 140 us (0.89)
  waiting for transfers between devices: 94.9 us -> 73.7 us
  blocking collectives: 4.58 us -> 9.52 us
    psum x1 -> x0, waiting for transfers between devices: 21.2 us -> none  [on_device(): summed = lax.psum(shard.astype(jnp.bfloat16), 'group')]
    all_gather x0 -> x1, blocking collectives: none -> 4.93 us  [on_device(): lax.all_gather(shard.astype(jnp.bfloat16), 'group')]
  transfers between devices with their start and end apart: 5 -> 4, of which waited for: 4 -> 3; matrix products, arithmetic and copies ran while one was open for 10% -> 11% of each run, Pallas kernels for 0% -> 0%
where the time goes in v1:
time: 140 us
  waiting for transfers between devices  73.7 us (53%)
  other arithmetic  16.9 us (12%)
  between operations  14.3 us (10%)
  starting transfers between devices  13.5 us (10%)
  blocking collectives  9.52 us (7%)
  local copies, waits for them, and re-layouts  6.11 us (4%)
  matrix products  5.54 us (4%)
    reduce_scatter x1, waiting for transfers between devices, on_device(): lax.psum_scatter(transpose_dot(stacked, pre_grad), 'dom', scatter_dimensi...  62.2 us
    all_to_all x1, starting transfers between devices, on_device(): lax.all_to_all(flags, 'dom', split_axis=0, concat_axis=0, tiled=True)  7.41 us
    all_to_all x1, waiting for transfers between devices, on_device(): lax.all_to_all(outgoing, 'dom', split_axis=0, concat_axis=0, tiled=True)  7.18 us
    all_to_all x1, starting transfers between devices, on_device(): lax.all_to_all(outgoing, 'dom', split_axis=0, concat_axis=0, tiled=True)  6.02 us
    all_gather x1, blocking collectives, on_device(): lax.all_gather(shard.astype(jnp.bfloat16), 'group')  4.93 us
    all_gather x1, blocking collectives, on_device(): all_negs = lax.all_gather(own_negs, 'group', axis=0, tiled=True)  4.58 us
    reduce_scatter x1, waiting for transfers between devices, on_device(): lax.psum_scatter((score_factor * transpose_dot(dscore, queries)).astype(j...  4.28 us
    scatter-add x1, other arithmetic, on_device(): emb_grad = emb_grad.at[query_rows[0]].add(query_grad)  3.71 us
  transfers between devices with their start and end apart: 4, of which 3 were waited for; matrix products, arithmetic and copies ran while one was open for 11% of the time, Pallas kernels for 0%

profile of v1, /device:TPU:0, one launch (start us, length us, event | category | flops | bytes accessed | tf_op | source)
XLA Modules:
  0.0 139.6 jit_solution(10528709249543655062)
XLA Ops:
  7.2 0.0 copy-start
  7.2 0.0 copy-start.2
  7.2 1.4 %compare_convert_fusion = bf16[16,1,16]{2,1,0:T(2,128)(2,1)} fusion(s32[16]{0:T(128)} %bitcast.57), kind=kLoop, calls=%fused_computation.38 | loop fusion | flops 512 | bytes 576 | tf_op jit(solution)/shard_map/convert_element_type | solution.py:48
  8.6 7.4 %all-to-all-start.1 = ((bf16[16,1,16]{2,1,0:T(2,128)(2,1)}), bf16[16,1,16]{2,1,0:T(2,128)(2,1)S(1)}, u32[]{:S(2)}, u32[]{:S(2)}) async-start(bf16[16,1,16]{2,1,0:T(2,128)(2,1)} %compare_convert_fusion), calls=%async_computation.1 | async-start | bytes 16384 | tf_op jit(solution)/shard_map/all_to_all | solution.py:53
  16.0 0.7 fusion.17
  16.7 0.7 compare_select_fusion.3
  17.4 0.1 reshape.231
  17.4 0.8 reshape_squeeze.3
  18.2 1.1 convert_reduce_fusion
  19.3 0.7 compare_select_fusion.1
  20.0 0.7 compare_select_fusion
  20.7 0.1 reshape.239
  20.8 1.4 %fusion.19 = f32[256,512]{1,0:T(8,128)S(1)} fusion(bf16[256,512]{1,0:T(8,128)(2,1)} %param.11, bf16[512,512]{1,0:T(8,128)(2,1)} %param.20), kind=kOutput, calls=%fused_computation.54 | convolution fusion | flops 134217728 | bytes 1310720 | tf_op jit(solution)/shard_map/dot_general | solution.py:68
  22.2 0.0 copy-done.2
  22.3 0.0 copy-start.3
  22.3 1.9 %gather_fusion.1 = bf16[256,512]{1,0:T(8,128)(2,1)} fusion(bf16[256,512]{1,0:T(8,128)(2,1)S(1)} %copy-done.2, s32[1024]{0:T(1024)S(1)} %pad_clamp_fusion.2), kind=kCustom, calls=%fused_computation.1 | custom fusion | bytes 525312 | tf_op jit(solution)/shard_map/gather | solution.py:47
  24.1 0.6 gather_fusion
  24.7 0.0 all-to-all-done.1
  24.8 6.0 %all-to-all-start = ((bf16[16,16,512]{2,1,0:T(8,128)(2,1)}), bf16[16,16,512]{2,1,0:T(8,128)(2,1)S(1)}, u32[]{:S(2)}, u32[]{:S(2)}) async-start(bf16[16,16,512]{2,1,0:T(8,128)(2,1)} %bitcast.10), calls=%async_computation | async-start | bytes 524288 | tf_op jit(solution)/shard_map/all_to_all | solution.py:52
  30.8 0.0 reduce-scatter.3.cloned.1.call-start
  30.8 0.0 copy-done.3
  30.9 0.3 fusion.9
  31.2 0.1 reshape.273
  31.3 2.3 %scatter_fusion.1 = f32[256]{0:T(256)S(1)} fusion(f32[256]{0:T(256)S(1)} %add_bitcast_fusion, s32[256]{0:T(256)S(1)} %bitcast.53, f32[256]{0:T(256)S(1)} %reshape.273), kind=kCustom, calls=%fused_computation.5 | custom fusion | flops 256 | bytes 4096 | tf_op jit(solution)/shard_map/scatter-add | solution.py:65
  33.6 7.2 %all-to-all-done = bf16[16,16,512]{2,1,0:T(8,128)(2,1)S(1)} async-done(((bf16[16,16,512]{2,1,0:T(8,128)(2,1)}), bf16[16,16,512]{2,1,0:T(8,128)(2,1)S(1)}, u32[]{:S(2)}, u32[]{:S(2)}) %all-to-all-start) | async-done | bytes 262176 | tf_op jit(solution)/shard_map/all_to_all | solution.py:52
  40.8 0.1 convert_multiply_fusion
  40.9 2.3 %scatter_fusion = f32[256,512]{1,0:T(8,128)S(1)} fusion(f32[256,512]{1,0:T(8,128)S(1)} %bitcast.47, s32[256]{0:T(256)S(1)} %bitcast.54, f32[256,512]{1,0:T(8,128)S(1)} %bitcast.50), kind=kCustom, calls=%fused_computation.4 | custom fusion | flops 131072 | bytes 1573888 | tf_op jit(solution)/shard_map/scatter-add | solution.py:64
  43.2 0.1 divide_convert_fusion
  43.3 0.0 copy-done
  43.3 0.4 multiply_reduce_fusion.1
  43.7 0.1 multiply_convert_fusion
  43.9 0.0 copy-start.1
  43.9 0.6 gather_fusion.3
  44.5 4.6 %all-gather = bf16[64,512]{1,0:T(8,128)(2,1)S(1)} all-gather(bf16[32,512]{1,0:T(8,128)(2,1)S(1)} %gather_fusion.3), channel_id=2, replica_groups=mesh['group'=2,'dom'=16] {'group'}, dimensions={0}, use_global_device_ids=true | all-gather | bytes 98304 | tf_op jit(solution)/shard_map/all_gather | solution.py:79
  49.1 0.0 copy-start.4
  49.1 2.0 %gather_fusion.2 = bf16[512,512]{1,0:T(8,128)(2,1)S(1)} fusion(bf16[256,512]{1,0:T(8,128)(2,1)S(1)} %multiply_convert_fusion, s32[1024]{0:T(1024)S(1)} %pad_clamp_fusion.1), kind=kCustom, calls=%fused_computation.2 | custom fusion | bytes 1050624 | tf_op jit(solution)/shard_map/gather | solution.py:73
  51.1 0.0 copy-done.1
  51.1 0.0 copy-done.4
  51.1 0.3 multiply_convert_fusion.1
  51.4 0.8 fusion.4
  52.3 0.0 reduce-scatter.3.cloned.1.call-update
  52.3 0.0 reduce-scatter.5.cloned.1.call-start
  52.3 0.3 convolution_multiply_fusion
  52.6 3.7 %scatter_custom_fusion.2 = f32[256,512]{1,0:T(8,128)S(1)} fusion(s32[512]{0:T(512)S(1)} %bitcast.56, f32[512,512]{1,0:T(8,128)S(1)} %convolution_multiply_fusion, f32[]{:T(128)} %constant.15.clone.1), kind=kCustom, calls=%fused_computation.31 | custom fusion | flops 262144 | bytes 524292 | tf_op jit(solution)/shard_map/scatter-add | solution.py:91
  56.4 4.3 %reduce-scatter.3.cloned.1.call-done = bf16[32,512]{1,0:T(8,128)(2,1)} async-done(((bf16[64,512]{1,0:T(8,128)(2,1)}), bf16[32,512]{1,0:T(8,128)(2,1)}) %reduce-scatter.3.cloned.1.call-update) | async-done | bytes 32784 | tf_op jit(solution)/shard_map/reduce_scatter | solution.py:84
  60.6 1.2 scatter_custom_fusion.3
  61.9 0.1 multiply_reduce_fusion
  62.0 2.0 %fusion.5 = f32[1024,512]{1,0:T(8,128)} fusion(bf16[256,512]{1,0:T(8,128)(2,1)S(1)} %divide_convert_fusion, bf16[256,512]{1,0:T(8,128)(2,1)S(1)} %copy-done.2, f32[256,512]{1,0:T(8,128)S(1)} %scatter_custom_fusion.3, f32[256,512]{1,0:T(8,128)S(1)} %get-tuple-element.3, f32[256]{0:T(256)S(1)} %broadcast_multiply_fusion, f32[256]{0:T(256)S(1)} %add_rsqrt_fusion), kind=kOutput, calls=%fused_computation.17 | convolution fusion | flops 270401536 | bytes 3672064 | tf_op jit(solution)/shard_map/dot_general | solution.py:20
  64.0 0.0 reduce-scatter.5.cloned.1.call-update
  64.0 62.2 %reduce-scatter.5.cloned.1.call-done = f32[64,512]{1,0:T(8,128)} async-done(((f32[1024,512]{1,0:T(8,128)}), f32[64,512]{1,0:T(8,128)}) %reduce-scatter.5.cloned.1.call-update) | async-done | bytes 131088 | tf_op jit(solution)/shard_map/reduce_scatter | solution.py:96
  126.2 0.9 convert_element_type.68
  127.2 4.9 %all-gather.1 = bf16[128,512]{1,0:T(8,128)(2,1)S(1)} all-gather(bf16[64,512]{1,0:T(8,128)(2,1)S(1)} %convert_element_type.68), channel_id=3, replica_groups=mesh['group'=2,'dom'=16] {'group'}, dimensions={0}, use_global_device_ids=true | all-gather | bytes 196608 | tf_op jit(solution)/shard_map/all_gather | solution.py:99
  132.1 0.7 reduce_sum.42
  (10 shorter events, 0.1 us)
Async XLA Ops:
  7.2 36.2 %copy-start = (bf16[512,512]{1,0:T(8,128)(2,1)S(1)}, bf16[512,512]{1,0:T(8,128)(2,1)}, u32[]{:S(2)}) copy-start(bf16[512,512]{1,0:T(8,128)(2,1)} %param.21) | copy-start | bytes 1572868
  7.2 15.1 %copy-start.2 = (bf16[256,512]{1,0:T(8,128)(2,1)S(1)}, bf16[256,512]{1,0:T(8,128)(2,1)}, u32[]{:S(2)}) copy-start(bf16[256,512]{1,0:T(8,128)(2,1)} %param.11) | copy-start | bytes 786436
  8.6 16.1 %all-to-all-start.1 = ((bf16[16,1,16]{2,1,0:T(2,128)(2,1)}), bf16[16,1,16]{2,1,0:T(2,128)(2,1)S(1)}, u32[]{:S(2)}, u32[]{:S(2)}) async-start(bf16[16,1,16]{2,1,0:T(2,128)(2,1)} %compare_convert_fusion), calls=%async_computation.1 | async-start | bytes 16384 | tf_op jit(solution)/shard_map/all_to_all | solution.py:53
  22.3 8.6 %copy-start.3 = (bf16[1,2,4,128,128]{4,3,2,1,0:T(8,128)(2,1)S(1)}, bf16[1,2,4,128,128]{4,3,2,1,0:T(8,128)(2,1)}, u32[]{:S(2)}) copy-start(bf16[1,2,4,128,128]{4,3,2,1,0:T(8,128)(2,1)} %param.13) | copy-start | bytes 786436
  24.8 16.0 %all-to-all-start = ((bf16[16,16,512]{2,1,0:T(8,128)(2,1)}), bf16[16,16,512]{2,1,0:T(8,128)(2,1)S(1)}, u32[]{:S(2)}, u32[]{:S(2)}) async-start(bf16[16,16,512]{2,1,0:T(8,128)(2,1)} %bitcast.10), calls=%async_computation | async-start | bytes 524288 | tf_op jit(solution)/shard_map/all_to_all | solution.py:52
  30.8 29.9 %reduce-scatter.3.cloned.1.call-start = ((), (), s32[]{:S(2)}) async-start(), calls=%async_computation.4 | async-start | bytes 98304 | tf_op jit(solution)/shard_map/reduce_scatter | solution.py:84
  43.9 7.2 %copy-start.1 = (bf16[256,512]{1,0:T(8,128)(2,1)}, bf16[256,512]{1,0:T(8,128)(2,1)S(1)}, u32[]{:S(2)}) copy-start(bf16[256,512]{1,0:T(8,128)(2,1)S(1)} %multiply_convert_fusion) | copy-start | bytes 786436
  49.1 2.0 %copy-start.4 = (s32[1,512]{1,0:T(1,128)S(1)}, s32[1,512]{1,0:T(1,128)}, u32[]{:S(2)}) copy-start(s32[1,512]{1,0:T(1,128)} %param.18) | copy-start | bytes 6148
  52.3 74.0 %reduce-scatter.5.cloned.1.call-start = ((), (), s32[]{:S(2)}) async-start(), calls=%async_computation.5 | async-start | bytes 2228224 | tf_op jit(solution)/shard_map/reduce_scatter | solution.py:96
Sparse Core Ops, SparseCore 0:
  52.4 8.1 reduce-scatter.2
  64.4 61.8 reduce-scatter.4
